TPU v7x, 512 devices: a whole 4x8x8 slice. The times are simulated.
512 devices in a mesh: space: 16 (over x, y_lo, core), term: 32 (over z, y_hi).
Axes of the slice: x: 4, y: 8 (y_hi: 4, y_lo: 2; y = y_hi * 2 + y_lo), z: 8, core: 2. Of those that a mesh axis runs over, the one named last changes fastest.
Arguments:
- right_modes: float32 [512, 64, 256], P(('space', 'term')), may hold values from -0.015625 to 0.015625
- adjoint_modes: float32 [512, 64, 256], P(('space', 'term')), may hold values from -6 to 6
- conductivity_terms: float32 [512, 256, 256], P('space', 'term'), may hold values from -6 to 6
Outputs:
- reduced_blocks: float32 [256, 4096], P('term', 'space')
All inputs are finite; a program needn't handle non-finite values.
Results may differ from a plain program's by a relative error of at most 0.000098.
Values sent between devices are 32-bit elements; how exact they have to be, the bound alone decides.
A program may use at most 64 MiB of HBM per device.

v0:
```python
import jax
import jax.numpy as jnp
from jax import lax
from jax.sharding import PartitionSpec as P

GY = 32


def extended(block, sides, width):
    for axis, dim in sides:
        count = lax.axis_size(axis)
        forward = [(i, i + 1) for i in range(count - 1)]
        backward = [(target, source) for source, target in forward]
        low = lax.ppermute(
            lax.slice_in_dim(block, block.shape[dim] - width, None, axis=dim), axis, forward
        )
        high = lax.ppermute(lax.slice_in_dim(block, 0, width, axis=dim), axis, backward)
        block = jnp.concatenate([low, block, high], axis=dim)
    return block


def shifted_cells(values, offset):
    zeros = jnp.zeros(values.shape[:-1] + (abs(offset),), jnp.float32)
    if offset > 0:
        return jnp.concatenate([values[..., offset:], zeros], axis=-1)
    return jnp.concatenate([zeros, values[..., :offset]], axis=-1)


def apply_terms(field_pad, coeff_pad, row_len):
    width = field_pad.shape[-1]
    column = jnp.arange(width) % row_len
    keep_next = (column != row_len - 1).astype(jnp.float32)
    keep_prev = (column != 0).astype(jnp.float32)
    centre = field_pad[None, 1:-1]
    coeff = coeff_pad[:, 1:-1, None, :]
    pairs = [
        (field_pad[None, 2:], coeff_pad[:, 2:, None, :]),
        (field_pad[None, :-2], coeff_pad[:, :-2, None, :]),
        (shifted_cells(centre, row_len), shifted_cells(coeff, row_len)),
        (shifted_cells(centre, -row_len), shifted_cells(coeff, -row_len)),
        (shifted_cells(centre, 1) * keep_next, shifted_cells(coeff, 1) * keep_next),
        (shifted_cells(centre, -1) * keep_prev, shifted_cells(coeff, -1) * keep_prev),
    ]
    result = jnp.zeros(coeff.shape[:2] + centre.shape[2:], jnp.float32)
    for other_field, other_coeff in pairs:
        result = result + 0.5 * (coeff + other_coeff) * (centre - other_field)
    return result


def assemble(field_pad, coeff_pad, adjoint, per_turn):
    modes = field_pad.shape[1]
    terms = coeff_pad.shape[1]
    ordered = jnp.moveaxis(coeff_pad, 1, 0)
    ordered = ordered.reshape((terms // per_turn, per_turn) + ordered.shape[1:])

    def one_block(coeff_block):
        image = apply_terms(field_pad, coeff_block, GY)
        return jnp.einsum("zrp,gzsp->grs", adjoint, image, precision=lax.Precision.HIGHEST)

    blocks = lax.map(one_block, ordered)
    return blocks.reshape(terms, modes * modes)


def local(right_modes, adjoint_modes, conductivity_terms):
    modes = right_modes.shape[1]
    slab_right, slab_adjoint = (
        lax.all_gather(right_modes, "term", axis=0, tiled=True),
        lax.all_gather(adjoint_modes, "term", axis=0, tiled=True),
    )
    stacked = jnp.concatenate([slab_right, conductivity_terms], axis=1)
    padded = extended(stacked, (("space", 0),), 1)
    partial_value = assemble(padded[:, :modes], padded[:, modes:], slab_adjoint, 1)
    return lax.psum_scatter(partial_value, "space", scatter_dimension=1, tiled=True)


def solution(mesh):
    placed = (
        P(("space", "term"), None, None),
        P(("space", "term"), None, None),
        P("space", "term", None),
    )
    return jax.shard_map(
        local, mesh=mesh, in_specs=placed, out_specs=P("term", "space"), check_vma=False
    )
```

profile of v0, /device:TPU:16, one launch (start us, length us, event | category | flops | bytes accessed | tf_op | source)
XLA Modules:
  0.0 315.2 jit_solution(1327591688766280557)
XLA Ops:
  8.1 93.2 %all-gather.3.cloned.1.call-done = f32[32,64,256]{2,1,0:T(8,128)} async-done(((f32[1,64,256]{2,1,0:T(8,128)}), f32[32,64,256]{2,1,0:T(8,128)}) %all-gather.3.cloned.1.call-update) | async-done | bytes 2097168 | tf_op jit(solution)/shard_map/all_gather | solution.py:67
  101.3 1.7 constant_dynamic-update-slice_fusion.2
  103.1 1.4 copy-done.3
  104.5 1.3 collective-permute-start.1
  105.8 3.0 collective-permute-start
  108.9 0.9 collective-permute-done
  109.7 1.0 maximum_bitcast_fusion
  111.0 1.3 copy-done.5
  112.3 2.5 fusion.38
  114.8 72.1 %all-gather.5.cloned.1.call-done = f32[32,64,256]{2,1,0:T(8,128)} async-done(((f32[1,64,256]{2,1,0:T(8,128)}), f32[32,64,256]{2,1,0:T(8,128)}) %all-gather.5.cloned.1.call-update) | async-done | bytes 2097168 | tf_op jit(solution)/shard_map/all_gather | solution.py:68
  186.9 58.4 %while.12 = (s32[]{:T(128)}, f32[8,1,64,64]{3,2,0,1:T(8,128)S(1)}, f32[8,1,34,256]{3,0,2,1:T(8,128)S(1)}, f32[32,64,256]{2,1,0:T(8,128)}, f32[32,64,256]{2,1,0:T...) while((s32[]{:T(128)}, f32[8,1,64,64]{3,2,0,1:T(8,128)S(1)}, ...), condition=%wide.region_1.2_spmd, body=%wide.region_0.1_spmd.sunk | while | flops 411683328 | bytes 63018424 | solution.py:60
  187.1 0.8 fusion.56
  187.9 0.8 fusion.57
  190.8 3.3 %fusion.61 = f32[1,1,64,64]{2,3,1,0:T(8,128)S(1)} fusion(f32[32,64,256]{2,1,0:T(8,128)S(1)} %copy-done.2, f32[32,64,256]{2,1,0:T(8,128)S(1)} %copy-done, f32[32,64,256]{2,1,0:T(8,128)S(1)} %copy-done.1, f32[1,32,64,255]{3,2,1,0:T(8,128)S(1)} %get-tuple-element.192, f32[1,32,64,255]{3,2,1,0:T(8,128)S(1)} %get-tuple-element.193, ...), kind=kOutput, calls=%fused_computation.24.clone.1 | convolution fusion | flops 411566080 | bytes 16992256 | tf_op jit(solution)/shard_map/while/body/eval_jaxpr/zrp,gzsp->grs/dot_general | solution.py:58
  194.4 0.8 fusion.56
  195.2 0.8 fusion.57
  198.1 3.3 %fusion.61 = f32[1,1,64,64]{2,3,1,0:T(8,128)S(1)} fusion(f32[32,64,256]{2,1,0:T(8,128)S(1)} %copy-done.2, f32[32,64,256]{2,1,0:T(8,128)S(1)} %copy-done, f32[32,64,256]{2,1,0:T(8,128)S(1)} %copy-done.1, f32[1,32,64,255]{3,2,1,0:T(8,128)S(1)} %get-tuple-element.192, f32[1,32,64,255]{3,2,1,0:T(8,128)S(1)} %get-tuple-element.193, ...), kind=kOutput, calls=%fused_computation.24.clone.1 | convolution fusion | flops 411566080 | bytes 16992256 | tf_op jit(solution)/shard_map/while/body/eval_jaxpr/zrp,gzsp->grs/dot_general | solution.py:58
  201.7 0.8 fusion.56
  202.5 0.8 fusion.57
  205.4 3.3 %fusion.61 = f32[1,1,64,64]{2,3,1,0:T(8,128)S(1)} fusion(f32[32,64,256]{2,1,0:T(8,128)S(1)} %copy-done.2, f32[32,64,256]{2,1,0:T(8,128)S(1)} %copy-done, f32[32,64,256]{2,1,0:T(8,128)S(1)} %copy-done.1, f32[1,32,64,255]{3,2,1,0:T(8,128)S(1)} %get-tuple-element.192, f32[1,32,64,255]{3,2,1,0:T(8,128)S(1)} %get-tuple-element.193, ...), kind=kOutput, calls=%fused_computation.24.clone.1 | convolution fusion | flops 411566080 | bytes 16992256 | tf_op jit(solution)/shard_map/while/body/eval_jaxpr/zrp,gzsp->grs/dot_general | solution.py:58
  209.0 0.8 fusion.56
  209.8 0.8 fusion.57
  212.7 3.3 %fusion.61 = f32[1,1,64,64]{2,3,1,0:T(8,128)S(1)} fusion(f32[32,64,256]{2,1,0:T(8,128)S(1)} %copy-done.2, f32[32,64,256]{2,1,0:T(8,128)S(1)} %copy-done, f32[32,64,256]{2,1,0:T(8,128)S(1)} %copy-done.1, f32[1,32,64,255]{3,2,1,0:T(8,128)S(1)} %get-tuple-element.192, f32[1,32,64,255]{3,2,1,0:T(8,128)S(1)} %get-tuple-element.193, ...), kind=kOutput, calls=%fused_computation.24.clone.1 | convolution fusion | flops 411566080 | bytes 16992256 | tf_op jit(solution)/shard_map/while/body/eval_jaxpr/zrp,gzsp->grs/dot_general | solution.py:58
  216.3 0.8 fusion.56
  217.1 0.8 fusion.57
  220.0 3.3 %fusion.61 = f32[1,1,64,64]{2,3,1,0:T(8,128)S(1)} fusion(f32[32,64,256]{2,1,0:T(8,128)S(1)} %copy-done.2, f32[32,64,256]{2,1,0:T(8,128)S(1)} %copy-done, f32[32,64,256]{2,1,0:T(8,128)S(1)} %copy-done.1, f32[1,32,64,255]{3,2,1,0:T(8,128)S(1)} %get-tuple-element.192, f32[1,32,64,255]{3,2,1,0:T(8,128)S(1)} %get-tuple-element.193, ...), kind=kOutput, calls=%fused_computation.24.clone.1 | convolution fusion | flops 411566080 | bytes 16992256 | tf_op jit(solution)/shard_map/while/body/eval_jaxpr/zrp,gzsp->grs/dot_general | solution.py:58
  223.6 0.8 fusion.56
  224.4 0.8 fusion.57
  227.3 3.3 %fusion.61 = f32[1,1,64,64]{2,3,1,0:T(8,128)S(1)} fusion(f32[32,64,256]{2,1,0:T(8,128)S(1)} %copy-done.2, f32[32,64,256]{2,1,0:T(8,128)S(1)} %copy-done, f32[32,64,256]{2,1,0:T(8,128)S(1)} %copy-done.1, f32[1,32,64,255]{3,2,1,0:T(8,128)S(1)} %get-tuple-element.192, f32[1,32,64,255]{3,2,1,0:T(8,128)S(1)} %get-tuple-element.193, ...), kind=kOutput, calls=%fused_computation.24.clone.1 | convolution fusion | flops 411566080 | bytes 16992256 | tf_op jit(solution)/shard_map/while/body/eval_jaxpr/zrp,gzsp->grs/dot_general | solution.py:58
  234.6 3.3 %fusion.61 = f32[1,1,64,64]{2,3,1,0:T(8,128)S(1)} fusion(f32[32,64,256]{2,1,0:T(8,128)S(1)} %copy-done.2, f32[32,64,256]{2,1,0:T(8,128)S(1)} %copy-done, f32[32,64,256]{2,1,0:T(8,128)S(1)} %copy-done.1, f32[1,32,64,255]{3,2,1,0:T(8,128)S(1)} %get-tuple-element.192, f32[1,32,64,255]{3,2,1,0:T(8,128)S(1)} %get-tuple-element.193, ...), kind=kOutput, calls=%fused_computation.24.clone.1 | convolution fusion | flops 411566080 | bytes 16992256 | tf_op jit(solution)/shard_map/while/body/eval_jaxpr/zrp,gzsp->grs/dot_general | solution.py:58
  241.9 3.3 %fusion.61 = f32[1,1,64,64]{2,3,1,0:T(8,128)S(1)} fusion(f32[32,64,256]{2,1,0:T(8,128)S(1)} %copy-done.2, f32[32,64,256]{2,1,0:T(8,128)S(1)} %copy-done, f32[32,64,256]{2,1,0:T(8,128)S(1)} %copy-done.1, f32[1,32,64,255]{3,2,1,0:T(8,128)S(1)} %get-tuple-element.192, f32[1,32,64,255]{3,2,1,0:T(8,128)S(1)} %get-tuple-element.193, ...), kind=kOutput, calls=%fused_computation.24.clone.1 | convolution fusion | flops 411566080 | bytes 16992256 | tf_op jit(solution)/shard_map/while/body/eval_jaxpr/zrp,gzsp->grs/dot_general | solution.py:58
  246.1 62.6 %reduce-scatter.2.cloned.1.call-done = f32[8,256]{1,0:T(8,128)} async-done(((f32[8,4096]{1,0:T(8,128)}), f32[8,256]{1,0:T(8,128)}) %reduce-scatter.2.cloned.1.call-update) | async-done | bytes 8208 | tf_op jit(solution)/shard_map/reduce_scatter | solution.py:73
  (150 shorter events, 23.7 us)
Async XLA Ops:
  6.5 94.8 %all-gather.3.cloned.1.call-start = ((), (), s32[]{:S(2)}) async-start(), calls=%async_computation.1 | async-start | bytes 2162688 | tf_op jit(solution)/shard_map/all_gather | solution.py:67
  7.3 179.7 %all-gather.5.cloned.1.call-start = ((), (), s32[]{:S(2)}) async-start(), calls=%async_computation.2 | async-start | bytes 2162688 | tf_op jit(solution)/shard_map/all_gather | solution.py:68
  8.0 95.0 %copy-start.6 = (f32[32,8,256]{2,1,0:T(8,128)S(1)}, f32[32,8,256]{2,1,0:T(8,128)}, u32[]{:S(2)}) copy-start(f32[32,8,256]{2,1,0:T(8,128)} %param.7) | copy-start | bytes 786436
  8.0 300.7 %reduce-scatter.2.cloned.1.call-start = ((), (), s32[]{:S(2)}) async-start(), calls=%async_computation.3 | async-start | bytes 139264 | tf_op jit(solution)/shard_map/reduce_scatter | solution.py:73
  104.5 4.4 %collective-permute-start.1 = (f32[1,72,256]{2,1,0:T(8,128)S(1)}, f32[1,72,256]{2,1,0:T(8,128)S(1)}, u32[]{:S(2)}, u32[]{:S(2)}) collective-permute-start(f32[1,72,256]{2,1,0:T(8,128)S(1)} %get-tuple-element.131), channel_id=1, source_target_pairs={{32,0},{64,32},{96,64},{128,96},{160,128},{192,160},{224,192},{256... | collective-permute-start | bytes 221192 | tf_op jit(solution)/shard_map/ppermute | solution.py:17
  105.8 3.9 %collective-permute-start = (f32[1,72,256]{2,1,0:T(8,128)S(1)}, f32[1,72,256]{2,1,0:T(8,128)S(1)}, u32[]{:S(2)}, u32[]{:S(2)}) collective-permute-start(f32[1,72,256]{2,1,0:T(8,128)S(1)} %get-tuple-element.130), channel_id=1, source_target_pairs={{0,32},{32,64},{64,96},{96,128},{128,160},{160,192},{192,224},{224... | collective-permute-start | bytes 221192 | tf_op jit(solution)/shard_map/ppermute | solution.py:14
  108.9 1.9 copy-start.4
  110.7 1.6 copy-start.5
  187.9 1.6 copy-start
  187.9 2.2 copy-start.1
  187.9 2.8 copy-start.2
  195.2 1.6 copy-start
  195.2 2.2 copy-start.1
  195.2 2.8 copy-start.2
  202.5 1.6 copy-start
  202.5 2.2 copy-start.1
  202.5 2.8 copy-start.2
  209.8 1.6 copy-start
  209.8 2.2 copy-start.1
  209.8 2.8 copy-start.2
  217.1 1.6 copy-start
  217.1 2.2 copy-start.1
  217.1 2.8 copy-start.2
  224.4 1.6 copy-start
  224.4 2.2 copy-start.1
  224.4 2.8 copy-start.2
  231.7 1.6 copy-start
  231.7 2.2 copy-start.1
  231.7 2.8 copy-start.2
  239.0 1.6 copy-start
  239.0 2.2 copy-start.1
  239.0 2.8 copy-start.2
  (1 other events, 1.4 us)
Sparse Core Ops, SparseCore 0:
  10.5 90.7 all-gather.2
  104.5 82.4 all-gather.4
  246.2 62.4 reduce-scatter.1
where the time goes:
time: 315 us
  waiting for transfers between devices  230 us (73%)
  local copies, waits for them, and re-layouts  35.1 us (11%)
  matrix products  26.7 us (8%)
  between operations  13.2 us (4%)
  other arithmetic  4.6 us (1%)
  starting transfers between devices  4.4 us (1%)
    all_gather x1, waiting for transfers between devices, local(): lax.all_gather(right_modes, 'term', axis=0, tiled=True)  93.2 us
    all_gather x1, waiting for transfers between devices, local(): lax.all_gather(adjoint_modes, 'term', axis=0, tiled=True)  72.1 us
    reduce_scatter x1, waiting for transfers between devices, local(): lax.psum_scatter(partial_value, 'space', scatter_dimension=1, tiled=True)  62.6 us
    dot_general x8, matrix products, one_block(): jnp.einsum('zrp,gzsp->grs', adjoint, image, precision=lax.Precision.HIGHEST)  26.7 us
    slice x32, local copies, waits for them, and re-layouts, shifted_cells(): return jnp.concatenate([values[..., offset:], zeros], axis=-1)  14 us
    while x48, local copies, waits for them, and re-layouts  13.6 us
  transfers between devices with their start and end apart: 5, of which 4 were waited for; matrix products, arithmetic and copies ran while one was open for 2% of the time, Pallas kernels for 0%

commit v1 on v0

--- a/solution.py
+++ b/solution.py
@@ -4,6 +4,11 @@
 from jax.sharding import PartitionSpec as P
 
 GY = 32
+
+
+def gather_over(shard, mesh_axis, d):
+    stack = jnp.stack([shard] * lax.axis_size(mesh_axis))
+    return jnp.concatenate(lax.all_to_all(stack, mesh_axis, 0, 0), axis=d)
 
 
 def extended(block, sides, width):
@@ -64,7 +69,7 @@
 def local(right_modes, adjoint_modes, conductivity_terms):
     modes = right_modes.shape[1]
     slab_right, slab_adjoint = (
-        lax.all_gather(right_modes, "term", axis=0, tiled=True),
+        gather_over(right_modes, "term", 0),
         lax.all_gather(adjoint_modes, "term", axis=0, tiled=True),
     )
     stacked = jnp.concatenate([slab_right, conductivity_terms], axis=1)

time: 315 us -> 268 us (0.85)
  waiting for transfers between devices: 230 us -> 166 us
  starting transfers between devices: 4.4 us -> 20.6 us
    all_gather x1 -> x0, waiting for transfers between devices: 93.2 us -> none  [local(): lax.all_gather(right_modes, 'term', axis=0, tiled=True)]
    all_to_all x0 -> x1, waiting for transfers between devices: none -> 59.9 us  [gather_over(): return jnp.concatenate(lax.all_to_all(stack, mesh_axis, 0, 0), axis=d)]
    all_gather x1, waiting for transfers between devices: 72.1 us -> 42.4 us  [local(): lax.all_gather(adjoint_modes, 'term', axis=0, tiled=True)]
    all_to_all x0 -> x1, starting transfers between devices: none -> 16.2 us  [gather_over(): return jnp.concatenate(lax.all_to_all(stack, mesh_axis, 0, 0), axis=d)]
    unnamed x9 -> x6, local copies, waits for them, and re-layouts: 4.49 us -> 0.3 us
where the time goes in v1:
time: 268 us
  waiting for transfers between devices  166 us (62%)
  local copies, waits for them, and re-layouts  33.7 us (13%)
  matrix products  27.3 us (10%)
  starting transfers between devices  20.6 us (8%)
  between operations  13.5 us (5%)
  other arithmetic  5.39 us (2%)
    reduce_scatter x1, waiting for transfers between devices, local(): lax.psum_scatter(partial_value, 'space', scatter_dimension=1, tiled=True)  62.6 us
    all_to_all x1, waiting for transfers between devices, gather_over(): return jnp.concatenate(lax.all_to_all(stack, mesh_axis, 0, 0), axis=d)  59.9 us
    all_gather x1, waiting for transfers between devices, local(): lax.all_gather(adjoint_modes, 'term', axis=0, tiled=True)  42.4 us
    dot_general x8, matrix products, one_block(): jnp.einsum('zrp,gzsp->grs', adjoint, image, precision=lax.Precision.HIGHEST)  27.3 us
    all_to_all x1, starting transfers between devices, gather_over(): return jnp.concatenate(lax.all_to_all(stack, mesh_axis, 0, 0), axis=d)  16.2 us
    slice x32, local copies, waits for them, and re-layouts, shifted_cells(): return jnp.concatenate([values[..., offset:], zeros], axis=-1)  14 us
    while x48, local copies, waits for them, and re-layouts  13.6 us
  transfers between devices with their start and end apart: 5, of which 4 were waited for; matrix products, arithmetic and copies ran while one was open for 2% of the time, Pallas kernels for 0%

profile of v1, /device:TPU:16, one launch (start us, length us, event | category | flops | bytes accessed | tf_op | source)
XLA Modules:
  0.0 267.8 jit_solution(13044951956243058376)
XLA Ops:
  6.5 2.4 stack.2
  8.9 16.2 %all-to-all-start = ((f32[32,1,64,256]{3,2,1,0:T(8,128)}), f32[32,1,64,256]{3,2,1,0:T(8,128)S(1)}, u32[]{:S(2)}, u32[]{:S(2)}) async-start(f32[32,1,64,256]{3,2,1,0:T(8,128)} %stack.2), calls=%async_computation | async-start | bytes 4194304 | tf_op jit(solution)/shard_map/all_to_all | solution.py:11
  25.9 59.9 %all-to-all-done = f32[32,1,64,256]{3,2,1,0:T(8,128)S(1)} async-done(((f32[32,1,64,256]{3,2,1,0:T(8,128)}), f32[32,1,64,256]{3,2,1,0:T(8,128)S(1)}, u32[]{:S(2)}, u32[]{:S(2)}) %all-to-all-start) | async-done | bytes 2097184 | tf_op jit(solution)/shard_map/all_to_all | solution.py:11
  85.8 1.3 collective-permute-start.1
  87.1 3.0 %collective-permute-start = (f32[1,72,256]{2,1,0:T(8,128)S(1)}, f32[1,72,256]{2,1,0:T(8,128)S(1)}, u32[]{:S(2)}, u32[]{:S(2)}) collective-permute-start(f32[1,72,256]{2,1,0:T(8,128)S(1)} %get-tuple-element.130), channel_id=1, source_target_pairs={{0,32},{32,64},{64,96},{96,128},{128,160},{160,192},{192,224},{224... | collective-permute-start | bytes 221192 | tf_op jit(solution)/shard_map/ppermute | solution.py:19
  90.2 0.9 collective-permute-done
  91.1 1.9 pad_maximum_fusion
  93.3 2.5 fusion.38
  95.9 42.4 %all-gather.2.cloned.1.call-done = f32[32,64,256]{2,1,0:T(8,128)} async-done(((f32[1,64,256]{2,1,0:T(8,128)}), f32[32,64,256]{2,1,0:T(8,128)}) %all-gather.2.cloned.1.call-update) | async-done | bytes 2097168 | tf_op jit(solution)/shard_map/all_gather | solution.py:73
  138.2 59.3 %while.12 = (s32[]{:T(128)}, f32[8,1,64,64]{3,2,0,1:T(8,128)S(1)}, f32[8,1,34,256]{3,0,2,1:T(8,128)S(1)}, f32[32,64,256]{2,1,0:T(8,128)}, f32[32,64,256]{2,1,0:T...) while((s32[]{:T(128)}, f32[8,1,64,64]{3,2,0,1:T(8,128)S(1)}, ...), condition=%wide.region_1.2_spmd, body=%wide.region_0.1_spmd.sunk | while | flops 411683328 | bytes 63018424 | solution.py:65
  138.5 0.8 fusion.55
  139.3 0.8 fusion.56
  142.1 3.4 %fusion.60 = f32[1,1,64,64]{2,3,1,0:T(8,128)S(1)} fusion(f32[32,64,256]{2,1,0:T(8,128)S(1)} %copy-done.2, f32[32,64,256]{2,1,0:T(8,128)S(1)} %copy-done, f32[32,64,256]{2,1,0:T(8,128)S(1)} %copy-done.1, f32[1,32,64,255]{3,2,1,0:T(8,128)S(1)} %get-tuple-element.192, f32[1,32,64,255]{3,2,1,0:T(8,128)S(1)} %get-tuple-element.193, ...), kind=kOutput, calls=%fused_computation.24.clone.1 | convolution fusion | flops 411566080 | bytes 16992256 | tf_op jit(solution)/shard_map/while/body/eval_jaxpr/zrp,gzsp->grs/dot_general | solution.py:63
  145.9 0.8 fusion.55
  146.7 0.8 fusion.56
  149.6 3.4 %fusion.60 = f32[1,1,64,64]{2,3,1,0:T(8,128)S(1)} fusion(f32[32,64,256]{2,1,0:T(8,128)S(1)} %copy-done.2, f32[32,64,256]{2,1,0:T(8,128)S(1)} %copy-done, f32[32,64,256]{2,1,0:T(8,128)S(1)} %copy-done.1, f32[1,32,64,255]{3,2,1,0:T(8,128)S(1)} %get-tuple-element.192, f32[1,32,64,255]{3,2,1,0:T(8,128)S(1)} %get-tuple-element.193, ...), kind=kOutput, calls=%fused_computation.24.clone.1 | convolution fusion | flops 411566080 | bytes 16992256 | tf_op jit(solution)/shard_map/while/body/eval_jaxpr/zrp,gzsp->grs/dot_general | solution.py:63
  153.3 0.8 fusion.55
  154.1 0.8 fusion.56
  157.0 3.4 %fusion.60 = f32[1,1,64,64]{2,3,1,0:T(8,128)S(1)} fusion(f32[32,64,256]{2,1,0:T(8,128)S(1)} %copy-done.2, f32[32,64,256]{2,1,0:T(8,128)S(1)} %copy-done, f32[32,64,256]{2,1,0:T(8,128)S(1)} %copy-done.1, f32[1,32,64,255]{3,2,1,0:T(8,128)S(1)} %get-tuple-element.192, f32[1,32,64,255]{3,2,1,0:T(8,128)S(1)} %get-tuple-element.193, ...), kind=kOutput, calls=%fused_computation.24.clone.1 | convolution fusion | flops 411566080 | bytes 16992256 | tf_op jit(solution)/shard_map/while/body/eval_jaxpr/zrp,gzsp->grs/dot_general | solution.py:63
  160.7 0.8 fusion.55
  161.6 0.8 fusion.56
  164.4 3.4 %fusion.60 = f32[1,1,64,64]{2,3,1,0:T(8,128)S(1)} fusion(f32[32,64,256]{2,1,0:T(8,128)S(1)} %copy-done.2, f32[32,64,256]{2,1,0:T(8,128)S(1)} %copy-done, f32[32,64,256]{2,1,0:T(8,128)S(1)} %copy-done.1, f32[1,32,64,255]{3,2,1,0:T(8,128)S(1)} %get-tuple-element.192, f32[1,32,64,255]{3,2,1,0:T(8,128)S(1)} %get-tuple-element.193, ...), kind=kOutput, calls=%fused_computation.24.clone.1 | convolution fusion | flops 411566080 | bytes 16992256 | tf_op jit(solution)/shard_map/while/body/eval_jaxpr/zrp,gzsp->grs/dot_general | solution.py:63
  168.1 0.8 fusion.55
  169.0 0.8 fusion.56
  171.8 3.4 %fusion.60 = f32[1,1,64,64]{2,3,1,0:T(8,128)S(1)} fusion(f32[32,64,256]{2,1,0:T(8,128)S(1)} %copy-done.2, f32[32,64,256]{2,1,0:T(8,128)S(1)} %copy-done, f32[32,64,256]{2,1,0:T(8,128)S(1)} %copy-done.1, f32[1,32,64,255]{3,2,1,0:T(8,128)S(1)} %get-tuple-element.192, f32[1,32,64,255]{3,2,1,0:T(8,128)S(1)} %get-tuple-element.193, ...), kind=kOutput, calls=%fused_computation.24.clone.1 | convolution fusion | flops 411566080 | bytes 16992256 | tf_op jit(solution)/shard_map/while/body/eval_jaxpr/zrp,gzsp->grs/dot_general | solution.py:63
  175.6 0.8 fusion.55
  179.2 3.4 %fusion.60 = f32[1,1,64,64]{2,3,1,0:T(8,128)S(1)} fusion(f32[32,64,256]{2,1,0:T(8,128)S(1)} %copy-done.2, f32[32,64,256]{2,1,0:T(8,128)S(1)} %copy-done, f32[32,64,256]{2,1,0:T(8,128)S(1)} %copy-done.1, f32[1,32,64,255]{3,2,1,0:T(8,128)S(1)} %get-tuple-element.192, f32[1,32,64,255]{3,2,1,0:T(8,128)S(1)} %get-tuple-element.193, ...), kind=kOutput, calls=%fused_computation.24.clone.1 | convolution fusion | flops 411566080 | bytes 16992256 | tf_op jit(solution)/shard_map/while/body/eval_jaxpr/zrp,gzsp->grs/dot_general | solution.py:63
  183.0 0.8 fusion.55
  186.7 3.4 %fusion.60 = f32[1,1,64,64]{2,3,1,0:T(8,128)S(1)} fusion(f32[32,64,256]{2,1,0:T(8,128)S(1)} %copy-done.2, f32[32,64,256]{2,1,0:T(8,128)S(1)} %copy-done, f32[32,64,256]{2,1,0:T(8,128)S(1)} %copy-done.1, f32[1,32,64,255]{3,2,1,0:T(8,128)S(1)} %get-tuple-element.192, f32[1,32,64,255]{3,2,1,0:T(8,128)S(1)} %get-tuple-element.193, ...), kind=kOutput, calls=%fused_computation.24.clone.1 | convolution fusion | flops 411566080 | bytes 16992256 | tf_op jit(solution)/shard_map/while/body/eval_jaxpr/zrp,gzsp->grs/dot_general | solution.py:63
  190.4 0.8 fusion.55
  194.1 3.4 %fusion.60 = f32[1,1,64,64]{2,3,1,0:T(8,128)S(1)} fusion(f32[32,64,256]{2,1,0:T(8,128)S(1)} %copy-done.2, f32[32,64,256]{2,1,0:T(8,128)S(1)} %copy-done, f32[32,64,256]{2,1,0:T(8,128)S(1)} %copy-done.1, f32[1,32,64,255]{3,2,1,0:T(8,128)S(1)} %get-tuple-element.192, f32[1,32,64,255]{3,2,1,0:T(8,128)S(1)} %get-tuple-element.193, ...), kind=kOutput, calls=%fused_computation.24.clone.1 | convolution fusion | flops 411566080 | bytes 16992256 | tf_op jit(solution)/shard_map/while/body/eval_jaxpr/zrp,gzsp->grs/dot_general | solution.py:63
  198.4 62.6 %reduce-scatter.2.cloned.1.call-done = f32[8,256]{1,0:T(8,128)} async-done(((f32[8,4096]{1,0:T(8,128)}), f32[8,256]{1,0:T(8,128)}) %reduce-scatter.2.cloned.1.call-update) | async-done | bytes 8208 | tf_op jit(solution)/shard_map/reduce_scatter | solution.py:78
  (146 shorter events, 22.6 us)
Async XLA Ops:
  8.9 76.9 %copy-start.5 = (f32[32,8,256]{2,1,0:T(8,128)S(1)}, f32[32,8,256]{2,1,0:T(8,128)}, u32[]{:S(2)}) copy-start(f32[32,8,256]{2,1,0:T(8,128)} %param.7) | copy-start | bytes 786436
  8.9 76.9 %all-to-all-start = ((f32[32,1,64,256]{3,2,1,0:T(8,128)}), f32[32,1,64,256]{3,2,1,0:T(8,128)S(1)}, u32[]{:S(2)}, u32[]{:S(2)}) async-start(f32[32,1,64,256]{3,2,1,0:T(8,128)} %stack.2), calls=%async_computation | async-start | bytes 4194304 | tf_op jit(solution)/shard_map/all_to_all | solution.py:11
  25.1 113.1 %all-gather.2.cloned.1.call-start = ((), (), s32[]{:S(2)}) async-start(), calls=%async_computation.2 | async-start | bytes 2162688 | tf_op jit(solution)/shard_map/all_gather | solution.py:73
  25.8 235.1 %reduce-scatter.2.cloned.1.call-start = ((), (), s32[]{:S(2)}) async-start(), calls=%async_computation.3 | async-start | bytes 139264 | tf_op jit(solution)/shard_map/reduce_scatter | solution.py:78
  85.8 5.3 %copy-start.3 = (f32[32,1,64,256]{3,2,1,0:T(8,128)}, f32[32,1,64,256]{3,2,1,0:T(8,128)S(1)}, u32[]{:S(2)}) copy-start(f32[32,1,64,256]{3,2,1,0:T(8,128)S(1)} %all-to-all-done) | copy-start | bytes 6291460
  85.8 4.4 %collective-permute-start.1 = (f32[1,72,256]{2,1,0:T(8,128)S(1)}, f32[1,72,256]{2,1,0:T(8,128)S(1)}, u32[]{:S(2)}, u32[]{:S(2)}) collective-permute-start(f32[1,72,256]{2,1,0:T(8,128)S(1)} %get-tuple-element.131), channel_id=1, source_target_pairs={{32,0},{64,32},{96,64},{128,96},{160,128},{192,160},{224,192},{256... | collective-permute-start | bytes 221192 | tf_op jit(solution)/shard_map/ppermute | solution.py:22
  87.1 3.9 %collective-permute-start = (f32[1,72,256]{2,1,0:T(8,128)S(1)}, f32[1,72,256]{2,1,0:T(8,128)S(1)}, u32[]{:S(2)}, u32[]{:S(2)}) collective-permute-start(f32[1,72,256]{2,1,0:T(8,128)S(1)} %get-tuple-element.130), channel_id=1, source_target_pairs={{0,32},{32,64},{64,96},{96,128},{128,160},{160,192},{192,224},{224... | collective-permute-start | bytes 221192 | tf_op jit(solution)/shard_map/ppermute | solution.py:19
  91.1 2.2 copy-start.4
  139.3 1.6 copy-start
  139.3 2.2 copy-start.1
  139.3 2.8 %copy-start.2 = (f32[32,64,256]{2,1,0:T(8,128)S(1)}, f32[32,64,256]{2,1,0:T(8,128)}, u32[]{:S(2)}) copy-start(f32[32,64,256]{2,1,0:T(8,128)} %get-tuple-element.231) | copy-start | bytes 6291460 | tf_op jit(solution)/shard_map/while
  146.7 1.6 copy-start
  146.7 2.2 copy-start.1
  146.7 2.8 %copy-start.2 = (f32[32,64,256]{2,1,0:T(8,128)S(1)}, f32[32,64,256]{2,1,0:T(8,128)}, u32[]{:S(2)}) copy-start(f32[32,64,256]{2,1,0:T(8,128)} %get-tuple-element.231) | copy-start | bytes 6291460 | tf_op jit(solution)/shard_map/while
  154.1 1.6 copy-start
  154.1 2.2 copy-start.1
  154.1 2.8 %copy-start.2 = (f32[32,64,256]{2,1,0:T(8,128)S(1)}, f32[32,64,256]{2,1,0:T(8,128)}, u32[]{:S(2)}) copy-start(f32[32,64,256]{2,1,0:T(8,128)} %get-tuple-element.231) | copy-start | bytes 6291460 | tf_op jit(solution)/shard_map/while
  161.5 1.6 copy-start
  161.5 2.2 copy-start.1
  161.5 2.8 %copy-start.2 = (f32[32,64,256]{2,1,0:T(8,128)S(1)}, f32[32,64,256]{2,1,0:T(8,128)}, u32[]{:S(2)}) copy-start(f32[32,64,256]{2,1,0:T(8,128)} %get-tuple-element.231) | copy-start | bytes 6291460 | tf_op jit(solution)/shard_map/while
  168.9 1.6 copy-start
  169.0 2.2 copy-start.1
  169.0 2.8 %copy-start.2 = (f32[32,64,256]{2,1,0:T(8,128)S(1)}, f32[32,64,256]{2,1,0:T(8,128)}, u32[]{:S(2)}) copy-start(f32[32,64,256]{2,1,0:T(8,128)} %get-tuple-element.231) | copy-start | bytes 6291460 | tf_op jit(solution)/shard_map/while
  176.4 1.6 copy-start
  176.4 2.2 copy-start.1
  176.4 2.8 %copy-start.2 = (f32[32,64,256]{2,1,0:T(8,128)S(1)}, f32[32,64,256]{2,1,0:T(8,128)}, u32[]{:S(2)}) copy-start(f32[32,64,256]{2,1,0:T(8,128)} %get-tuple-element.231) | copy-start | bytes 6291460 | tf_op jit(solution)/shard_map/while
  183.8 1.6 copy-start
  183.8 2.2 copy-start.1
  183.8 2.8 %copy-start.2 = (f32[32,64,256]{2,1,0:T(8,128)S(1)}, f32[32,64,256]{2,1,0:T(8,128)}, u32[]{:S(2)}) copy-start(f32[32,64,256]{2,1,0:T(8,128)} %get-tuple-element.231) | copy-start | bytes 6291460 | tf_op jit(solution)/shard_map/while
  191.2 1.6 copy-start
  191.2 2.2 copy-start.1
  191.2 2.8 %copy-start.2 = (f32[32,64,256]{2,1,0:T(8,128)S(1)}, f32[32,64,256]{2,1,0:T(8,128)}, u32[]{:S(2)}) copy-start(f32[32,64,256]{2,1,0:T(8,128)} %get-tuple-element.231) | copy-start | bytes 6291460 | tf_op jit(solution)/shard_map/while
Sparse Core Ops, SparseCore 0:
  29.1 109.1 all-gather.1
  198.5 62.4 reduce-scatter.1
